TPU v7x, 32 devices: a whole 2x2x4 slice. The times are simulated.
32 devices in a mesh: groups: 2 (over x), seq: 16 (over z, y, core).
Axes of the slice: x: 2, y: 2, z: 4, core: 2. Of those that a mesh axis runs over, the one named last changes fastest.
Arguments:
- hidden_states: bfloat16 [37, 512, 2560], P(None, ('groups', 'seq')), parts along dimension 1, may hold values from -80 to 80
- layer_mix: float32 [37], replicated, may hold values from 0.05 to 1
- norm_gain: float32 [2560], replicated, may hold values from 0.1 to 1.9
- norm_bias: float32 [2560], replicated, may hold values from -3 to 3
- proj_in: bfloat16 [2560, 1024], replicated, may hold values from -0.125 to 0.125
- proj_in_bias: float32 [1024], replicated, may hold values from -3 to 3
- proj_out: bfloat16 [1024, 1024], replicated, may hold values from -0.1875 to 0.1875
- proj_out_bias: float32 [1024], replicated, may hold values from -3 to 3
- residue_tokens: int32 [512], P(('groups', 'seq')), parts along dimension 0, may hold values from 0 to 22
- residue_table: float32 [23, 1024], replicated, may hold values from -5 to 5
- pair_norm_gain: float32 [1024], replicated, may hold values from 0.1 to 1.9
- pair_norm_bias: float32 [1024], replicated, may hold values from -3 to 3
- qk_weight: bfloat16 [1024, 128], replicated, may hold values from -0.1875 to 0.1875
- qk_bias: float32 [128], replicated, may hold values from -3 to 3
- pair_weight: bfloat16 [128, 128], replicated, may hold values from -0.75 to 0.75
- relpos_bins: int32 [512, 256], P(('groups', 'seq')), parts along dimension 0, may hold values from 0 to 65
- relpos_table: float32 [66, 128], replicated, may hold values from -5 to 5
- chain_ids: int32 [512], P(('groups', 'seq')), parts along dimension 0, may hold values from 0 to 7, never falling along the last dimension, each value on 1 to 64 neighbouring positions
- chain_table: float32 [2, 128], replicated, may hold values from -5 to 5
Outputs:
- single: bfloat16 [512, 1024], P(('groups', 'seq')), parts along dimension 0
- pair: bfloat16 [512, 256, 128], P(('groups', 'seq')), parts along dimension 0
There are 2 independent parts, one for each index of `groups`. A program takes and returns all parts, laid end to end along the dimension named above; an argument that names none is the same for every part. Nothing has to cross between parts.
Inputs may be any that keep to these rules, and one draw needn't show every extreme that they name: `chain_ids`: chain numbers never fall along the residues; each chain has at most 64 residues.
All inputs are finite; a program needn't handle non-finite values.
Results may differ from a plain program's by a relative error of at most 0.0067.
Values may be sent and summed in bfloat16 or wider, within the bound.
A program may use at most 64 MiB of HBM per device.

v0:
```python
import functools

import jax
import jax.numpy as jnp
from jax import lax
from jax.experimental import pallas as pl
from jax.experimental.pallas import tpu as pltpu
from jax.sharding import PartitionSpec as P

epsilon = 1e-05
F32 = jnp.float32
BF16 = jnp.bfloat16
LANES = 128


def layer_norm(values, weight_gain, weight_bias):
    center = values - jnp.mean(values, axis=-1, keepdims=True)
    spread = jnp.mean(center * center, axis=-1, keepdims=True)
    return center * lax.rsqrt(spread + epsilon) * weight_gain + weight_bias


def split_hi_lo(values):
    hi = values.astype(BF16)
    lo = (values - hi.astype(F32)).astype(BF16)
    return hi, lo


def column_of(scalars_ref, count, shape):
    rows = lax.broadcasted_iota(jnp.int32, shape, 0)
    out = jnp.zeros(shape, jnp.int32)
    for i in range(count):
        out = jnp.where(rows == i, scalars_ref[i], out)
    return out


def as_row(tiles_ref):
    return jnp.concatenate(
        [tiles_ref[pl.ds(r, 1), :] for r in range(tiles_ref.shape[0])], axis=1
    )


def kernel(
    n,
    parts,
    h_chunks,
    k_chunks,
    hidden_hbm,
    mix_hbm,
    norm_gain_hbm,
    norm_bias_hbm,
    proj_in_hbm,
    proj_in_bias_hbm,
    proj_out_hbm,
    proj_out_bias_hbm,
    tokens_hbm,
    residue_table_hbm,
    pair_gain_hbm,
    pair_bias_hbm,
    qk_weight_hbm,
    qk_bias_hbm,
    pair_weight_hbm,
    bins_hbm,
    relpos_hbm,
    chain_hbm,
    chain_table_hbm,
    single_ref,
    pair_ref,
    base_ref,
    last_keys_ref,
    q_ref,
    weight_ref,
    hidden_v,
    mix_s,
    norm_gain_v,
    norm_bias_v,
    proj_in_v,
    proj_in_bias_v,
    proj_out_v,
    proj_out_bias_v,
    tokens_s,
    residue_table_v,
    pair_gain_v,
    pair_bias_v,
    qk_weight_v,
    qk_bias_v,
    pair_weight_v,
    bins_v,
    relpos_v,
    chain_s,
    chain_table_v,
    mixture_v,
    residue_v,
    tables_v,
    base_v,
    keys_v,
    copy_sems,
    send_sems,
    recv_sems,
):
    me = lax.axis_index("seq")
    barrier = pltpu.get_barrier_semaphore()
    nst, tok, d = hidden_v.shape
    inner = pair_weight_v.shape[0] // 2
    length = bins_v.shape[1]
    cz = pair_weight_v.shape[1]
    nbins = relpos_v.shape[0]
    nbins_pad = tables_v.shape[0] // 2
    per = n // parts
    width = per * tok
    first = length - width

    copies = []

    def fetch(src, dst):
        copy = pltpu.make_async_copy(src, dst, copy_sems.at[len(copies)])
        copy.start()
        copies.append(copy)
        return copy

    mix_copy = fetch(mix_hbm, mix_s)
    h_width = d // h_chunks
    h_copies = [
        fetch(
            hidden_hbm.at[:, :, pl.ds(c * h_width, h_width)],
            hidden_v.at[:, :, pl.ds(c * h_width, h_width)],
        )
        for c in range(h_chunks)
    ]
    tok_copy = fetch(tokens_hbm, tokens_s)
    chain_copy = fetch(chain_hbm, chain_s)
    norm_copies = [fetch(norm_gain_hbm, norm_gain_v), fetch(norm_bias_hbm, norm_bias_v)]
    table_copy = fetch(residue_table_hbm, residue_table_v)
    k_depth = d // k_chunks
    in_copies = [
        fetch(
            proj_in_hbm.at[pl.ds(c * k_depth, k_depth), :],
            proj_in_v.at[pl.ds(c * k_depth, k_depth), :],
        )
        for c in range(k_chunks)
    ]
    bias_copies = [fetch(proj_in_bias_hbm, proj_in_bias_v), fetch(proj_out_bias_hbm, proj_out_bias_v)]
    o_chunks = 4 if proj_out_v.shape[0] % (4 * LANES) == 0 else 1
    o_depth = proj_out_v.shape[0] // o_chunks
    out_copies = [
        fetch(
            proj_out_hbm.at[pl.ds(c * o_depth, o_depth), :],
            proj_out_v.at[pl.ds(c * o_depth, o_depth), :],
        )
        for c in range(o_chunks)
    ]
    qk_copies = [
        fetch(pair_gain_hbm, pair_gain_v),
        fetch(pair_bias_hbm, pair_bias_v),
        fetch(qk_weight_hbm, qk_weight_v),
        fetch(qk_bias_hbm, qk_bias_v),
    ]
    pair_copies = [
        fetch(pair_weight_hbm, pair_weight_v),
        fetch(bins_hbm, bins_v),
        fetch(relpos_hbm, relpos_v),
        fetch(chain_table_hbm, chain_table_v),
    ]

    for step in range(1, n):
        pl.semaphore_signal(
            barrier,
            inc=1,
            device_id={"seq": lax.rem(me + step, n)},
            device_id_type=pl.DeviceIdType.MESH,
        )

    mix_copy.wait()
    for c in range(h_chunks):
        h_copies[c].wait()
        cols = pl.ds(c * h_width, h_width)
        total = mix_s[0] * hidden_v[0, :, cols].astype(F32)
        for k in range(1, nst):
            total = total + mix_s[k] * hidden_v[k, :, cols].astype(F32)
        mixture_v[:, cols] = total

    for copy in norm_copies:
        copy.wait()
    normed = layer_norm(mixture_v[...], as_row(norm_gain_v), as_row(norm_bias_v)).astype(BF16)

    tok_copy.wait()
    chain_copy.wait()
    table_copy.wait()
    for i in range(tok):
        residue_v[pl.ds(i, 1), :] = residue_table_v[pl.ds(tokens_s[i], 1), :]

    hidden = jnp.zeros((tok, proj_in_v.shape[1]), F32)
    for c in range(k_chunks):
        in_copies[c].wait()
        hidden = hidden + jnp.dot(
            normed[:, c * k_depth : (c + 1) * k_depth],
            proj_in_v[pl.ds(c * k_depth, k_depth), :],
            preferred_element_type=F32,
        )
    for copy in bias_copies:
        copy.wait()
    hidden = jnp.maximum(hidden + proj_in_bias_v[...], 0.0).astype(BF16)
    single_f = proj_out_bias_v[...] + residue_v[...]
    for c in range(o_chunks):
        out_copies[c].wait()
        single_f = single_f + jnp.dot(
            hidden[:, c * o_depth : (c + 1) * o_depth],
            proj_out_v[pl.ds(c * o_depth, o_depth), :],
            preferred_element_type=F32,
        )
    for copy in qk_copies:
        copy.wait()
    pair_in = layer_norm(single_f, pair_gain_v[...], pair_bias_v[...]).astype(BF16)
    query_key = jnp.dot(pair_in, qk_weight_v[...], preferred_element_type=F32) + qk_bias_v[...]

    span = (LANES - inner) // 2
    lane = lax.broadcasted_iota(jnp.int32, (tok, LANES), 1)
    chains = column_of(chain_s, tok, (tok, LANES))
    onehot = jnp.where(
        (lane == chains + inner) | (lane == chains + (inner + span)), 1.0, 0.0
    ).astype(F32)
    q_rows = jnp.where(lane < inner, query_key, onehot).astype(BF16)
    k_rows = jnp.where(
        lane < inner, pltpu.roll(query_key, LANES - inner, 1), onehot
    ).astype(BF16)
    keys_v[me] = k_rows

    pl.semaphore_wait(barrier, n - 1)
    def push(place):
        target = jnp.where(2 * me >= n, place, n - 1 - place)
        return target, pltpu.make_async_remote_copy(
            src_ref=keys_v.at[me],
            dst_ref=keys_v.at[me],
            send_sem=send_sems.at[place],
            recv_sem=recv_sems.at[me],
            device_id={"seq": target},
            device_id_type=pl.DeviceIdType.MESH,
        )

    for place in range(n):
        target, copy = push(place)
        pl.when(target != me)(copy.start)

    q_ref[...] = q_rows
    single_ref[...] = single_f.astype(BF16)
    for copy in pair_copies:
        copy.wait()
    pair_weight = pair_weight_v[...]
    low_weight = pair_weight[inner:]
    row_diff = jnp.dot(q_rows[:, :inner], low_weight, preferred_element_type=F32)
    chain_base = chain_table_v[pl.ds(0, 1), :]
    chain_hi, chain_lo = split_hi_lo(chain_table_v[pl.ds(1, 1), :] - chain_base)
    weight = jnp.concatenate(
        [
            pair_weight[:inner],
            jnp.broadcast_to(chain_hi, (span, cz)),
            jnp.broadcast_to(chain_lo, (span, cz)),
        ],
        axis=0,
    )
    weight_ref[...] = weight
    tables_v[...] = jnp.zeros_like(tables_v)
    hi, lo = split_hi_lo(relpos_v[...])
    tables_v[pl.ds(0, nbins), :] = hi
    tables_v[pl.ds(nbins_pad, nbins), :] = lo
    tables = tables_v[...]
    row_base = row_diff + chain_base
    bins = jnp.concatenate(
        [bins_v[...], jnp.zeros((LANES - tok, length), jnp.int32)], axis=0
    )
    bins_t = bins.T
    bin_lane = lax.broadcasted_iota(jnp.int32, (length, nbins_pad), 1)
    for i in range(tok):
        hot = jnp.where(bins_t[:, i : i + 1] == bin_lane, 1.0, 0.0).astype(BF16)
        base = (
            jnp.dot(
                jnp.concatenate([hot, hot], axis=1), tables, preferred_element_type=F32
            )
            + row_base[i : i + 1]
        )
        base_v[i] = base[:first]
        base_ref[i] = base[first:]

    for part in range(parts):
        for source in range(part * per, (part + 1) * per):
            step = lax.rem(me - source + n, n)

            @pl.when(step > 0)
            def _():
                pltpu.make_async_remote_copy(
                    src_ref=keys_v.at[source],
                    dst_ref=keys_v.at[source],
                    send_sem=send_sems.at[source],
                    recv_sem=recv_sems.at[source],
                    device_id={"seq": lax.rem(me + 1, n)},
                    device_id_type=pl.DeviceIdType.MESH,
                ).wait_recv()

        keys = keys_v[pl.ds(part * per, per)].reshape(width, LANES)
        if part == parts - 1:
            last_keys_ref[...] = keys
        else:
            col_diff = jnp.dot(keys[:, :inner], low_weight, preferred_element_type=F32)
            for i in range(tok):
                pair_ref[i, pl.ds(part * width, width), :] = (
                    jnp.dot(keys * q_rows[i : i + 1], weight, preferred_element_type=F32)
                    + base_v[i, pl.ds(part * width, width), :]
                    - col_diff
                ).astype(BF16)
    for place in range(n):
        target, copy = push(place)
        pl.when(target != me)(copy.wait_send)


def finish(
    single_ref, pair_ref, base_ref, keys_ref, q_ref, weight_ref, low_weight_ref,
    single_hbm, pair_hbm, last_v, sems,
):
    tok, width, cz = base_ref.shape
    first = pair_ref.shape[1]
    inner = low_weight_ref.shape[0] // 2
    copies = [pltpu.make_async_copy(single_ref, single_hbm, sems.at[0])]
    copies[0].start()
    if first:
        early = pltpu.make_async_copy(
            pair_ref, pair_hbm.at[:, pl.ds(0, first), :], sems.at[1]
        )
        early.start()
        copies.append(early)
    keys = keys_ref[...]
    weight = weight_ref[...]
    col_diff = jnp.dot(
        keys[:, :inner], low_weight_ref[pl.ds(inner, inner), :], preferred_element_type=F32
    )
    for i in range(tok):
        last_v[i] = (
            jnp.dot(keys * q_ref[pl.ds(i, 1), :], weight, preferred_element_type=F32)
            + base_ref[i]
            - col_diff
        ).astype(BF16)
    late = pltpu.make_async_copy(
        last_v, pair_hbm.at[:, pl.ds(first, width), :], sems.at[2]
    )
    late.start()
    copies.append(late)
    for copy in copies:
        copy.wait()


def shards(n, *args):
    (hidden, mix, norm_gain, norm_bias, proj_in, proj_in_bias, proj_out, proj_out_bias,
     tokens, residue_table, pair_gain, pair_bias, qk_weight, qk_bias, pair_weight,
     bins, relpos, chain, chain_table) = args
    row = lambda a: a.reshape(1, a.shape[0])
    tiles = lambda a: a.reshape(a.shape[0] // LANES, LANES)
    args = (hidden, mix, tiles(norm_gain), tiles(norm_bias), proj_in, row(proj_in_bias),
            proj_out, row(proj_out_bias), tokens, residue_table, row(pair_gain),
            row(pair_bias), qk_weight, row(qk_bias), pair_weight, bins, relpos, chain,
            chain_table)
    args = tuple(pltpu.with_memory_space_constraint(a, pltpu.HBM) for a in args)
    smem = (1, 8, 17)
    staged = [
        (pltpu.SMEM if i in smem else pltpu.VMEM)(a.shape, a.dtype) for i, a in enumerate(args)
    ]
    nst, tok, d = hidden.shape
    cs = proj_out.shape[1]
    cz = pair_weight.shape[1]
    length = bins.shape[1]
    nbins_pad = -(-relpos.shape[0] // LANES) * LANES
    h_chunks = k_chunks = 5 if d % (5 * LANES) == 0 else 1
    n_copies = len(args) + 1 + h_chunks + k_chunks
    parts = 4 if n % 4 == 0 else 2
    width = length // parts
    first = length - width
    vmem = pl.BlockSpec(memory_space=pltpu.VMEM)
    hbm = pl.BlockSpec(memory_space=pltpu.HBM)
    mid = pl.pallas_call(
        functools.partial(kernel, n, parts, h_chunks, k_chunks),
        out_shape=(
            jax.ShapeDtypeStruct((tok, cs), BF16),
            jax.ShapeDtypeStruct((tok, first, cz), BF16),
            jax.ShapeDtypeStruct((tok, width, cz), F32),
            jax.ShapeDtypeStruct((width, LANES), BF16),
            jax.ShapeDtypeStruct((tok, LANES), BF16),
            jax.ShapeDtypeStruct((LANES, cz), BF16),
        ),
        in_specs=[hbm] * len(args),
        out_specs=(vmem,) * 6,
        scratch_shapes=staged
        + [
            pltpu.VMEM((tok, d), F32),
            pltpu.VMEM((tok, cs), F32),
            pltpu.VMEM((2 * nbins_pad, cz), BF16),
            pltpu.VMEM((tok, first, cz), F32),
            pltpu.VMEM((n, tok, LANES), BF16),
            pltpu.SemaphoreType.DMA((n_copies,)),
            pltpu.SemaphoreType.DMA((n,)),
            pltpu.SemaphoreType.DMA((n,)),
        ],
        compiler_params=pltpu.CompilerParams(
            collective_id=0, has_side_effects=True, vmem_limit_bytes=40 << 20
        ),
    )(*args)
    return pl.pallas_call(
        finish,
        out_shape=(
            jax.ShapeDtypeStruct((tok, cs), BF16),
            jax.ShapeDtypeStruct((tok, length, cz), BF16),
        ),
        in_specs=[vmem] * 7,
        out_specs=(hbm, hbm),
        scratch_shapes=[
            pltpu.VMEM((tok, width, cz), BF16),
            pltpu.SemaphoreType.DMA((3,)),
        ],
        compiler_params=pltpu.CompilerParams(vmem_limit_bytes=16 << 20),
    )(*mid, pair_weight)


def solution(mesh):
    in_specs = (
        P(None, ("groups", "seq"), None),
        P(),
        P(),
        P(),
        P(),
        P(),
        P(),
        P(),
        P(("groups", "seq")),
        P(),
        P(),
        P(),
        P(),
        P(),
        P(),
        P(("groups", "seq"), None),
        P(),
        P(("groups", "seq")),
        P(),
    )
    out_specs = (P(("groups", "seq"), None), P(("groups", "seq"), None, None))
    return jax.shard_map(
        functools.partial(shards, mesh.shape["seq"]),
        mesh=mesh,
        in_specs=in_specs,
        out_specs=out_specs,
        check_vma=False,
    )
```

profile of v0, /device:TPU:0, one launch (start us, length us, event | category | flops | bytes accessed | tf_op | source)
XLA Modules:
  0.0 14.5 jit_solution(18025750292411664598)
XLA Ops:
  0.6 0.0 copy-start
  0.6 12.8 %shard_map.194 = (bf16[16,1024]{1,0:T(8,128)(2,1)S(1)}, bf16[16,192,128]{2,1,0:T(8,128)(2,1)S(1)}, f32[16,64,128]{2,1,0:T(8,128)S(1)}, bf16[64,128]{1,0:T(8,128)...) custom-call(bf16[37,16,2560]{2,1,0:T(8,128)(2,1)} %hidden_hbm.1, f32[37]{0:T(128)} %mix_hbm.1, ...), custom_call_target="tpu_custom_call" | custom-call | tf_op jit(solution)/shard_map/pallas_call | solution.py:376
  13.5 0.0 copy-done
  13.5 1.0 %shard_map.195 = (bf16[16,1024]{1,0:T(8,128)(2,1)}, bf16[16,256,128]{2,1,0:T(8,128)(2,1)}) custom-call(bf16[16,1024]{1,0:T(8,128)(2,1)S(1)} %get-tuple-element.8.single_ref, bf16[16,192,128]{2,1,0:T(8,128)(2,1)S(1)} %get-tuple-element.9.pair_ref, f32[16,64,128]{2,1,0:T(8,128)S(1)} %get-tuple-element.10.base_ref, ...), custom_call_target="tpu_custom_call" | custom-call | tf_op jit(solution)/shard_map/pallas_call | solution.py:403
Async XLA Ops:
  0.6 12.9 %copy-start = (bf16[128,128]{1,0:T(8,128)(2,1)S(1)}, bf16[128,128]{1,0:T(8,128)(2,1)}, u32[]{:S(2)}) copy-start(bf16[128,128]{1,0:T(8,128)(2,1)} %low_weight_ref.1) | copy-start | bytes 98308
where the time goes:
time: 14.7 us; the launch traced here: 14.5 us
  Pallas kernels  13.8 us (94%)
  between operations  0.66 us (4%)
    pallas_call x1, Pallas kernels, shards(): pl.pallas_call(functools.partial(kernel, n, parts, h_chunks, k_chunks), o...  12.8 us
    pallas_call x1, Pallas kernels, shards(): pl.pallas_call(finish, out_shape=(jax.ShapeDtypeStruct((tok, cs), BF16),...  1 us

commit v1 on v0

v1 whole, which is shorter than its diff:
```python
import functools

import jax
import jax.numpy as jnp
from jax import lax
from jax.experimental import pallas as pl
from jax.experimental.pallas import tpu as pltpu
from jax.sharding import PartitionSpec as P

epsilon = 1e-05
F32 = jnp.float32
BF16 = jnp.bfloat16
LANES = 128
MESH = pl.DeviceIdType.MESH


def layer_norm(values, weight_gain, weight_bias):
    center = values - jnp.mean(values, axis=-1, keepdims=True)
    spread = jnp.mean(center * center, axis=-1, keepdims=True)
    return center * lax.rsqrt(spread + epsilon) * weight_gain + weight_bias


def split_hi_lo(values):
    hi = values.astype(BF16)
    lo = (values - hi.astype(F32)).astype(BF16)
    return hi, lo


def split_three(values):
    hi = values.astype(BF16)
    rest = values - hi.astype(F32)
    mid = rest.astype(BF16)
    low = (rest - mid.astype(F32)).astype(BF16)
    return jnp.concatenate([hi, mid, low], axis=0)


def sum_three(stacked):
    rows = stacked.shape[0] // 3
    return stacked[:rows] + (stacked[rows : 2 * rows] + stacked[2 * rows :])


def column_of(scalars_ref, count, shape):
    rows = lax.broadcasted_iota(jnp.int32, shape, 0)
    out = jnp.zeros(shape, jnp.int32)
    for i in range(count):
        out = jnp.where(rows == i, scalars_ref[i], out)
    return out


def as_row(tiles):
    return jnp.concatenate([tiles[r : r + 1] for r in range(tiles.shape[0])], axis=1)


def pair_block(keys, q_rows, weight, rows):
    lhs = [jnp.concatenate([keys * q_rows[i : i + 1], keys], axis=1) for i in rows]
    return jnp.dot(jnp.concatenate(lhs, axis=0), weight, preferred_element_type=F32)


def kernel(
    n,
    parts,
    h_chunks,
    k_chunks,
    o_chunks,
    hidden_hbm,
    mix_hbm,
    norm_gain_hbm,
    norm_bias_hbm,
    proj_in_hbm,
    proj_in_bias_hbm,
    proj_out_hbm,
    proj_out_bias_hbm,
    tokens_hbm,
    residue_table_hbm,
    pair_gain_hbm,
    pair_bias_hbm,
    qk_weight_hbm,
    qk_bias_hbm,
    pair_weight_hbm,
    bins_hbm,
    relpos_hbm,
    chain_hbm,
    chain_table_hbm,
    single_ref,
    pair_ref,
    base_ref,
    last_keys_ref,
    q_ref,
    weight_ref,
    hidden_v,
    mix_s,
    norm_v,
    proj_in_v,
    vec_v,
    proj_out_v,
    tokens_s,
    residue_table_v,
    qk_weight_v,
    qk_bias_v,
    pair_weight_v,
    bins_v,
    relpos_v,
    chain_s,
    chain_table_v,
    mixture_v,
    residue_v,
    tables_v,
    base_v,
    keys_v,
    copy_sems,
    send_sem,
    recv_sems,
):
    me = lax.axis_index("seq")
    barrier = pltpu.get_barrier_semaphore()
    nst, tok, d = hidden_v.shape
    inner = pair_weight_v.shape[0] // 2
    length = bins_v.shape[1]
    cz = pair_weight_v.shape[1]
    nbins = relpos_v.shape[0]
    nbins_pad = tables_v.shape[0] // 2
    per = n // parts
    width = per * tok
    first = length - width
    n_sems = [0]

    def fetch(*pairs):
        sem = copy_sems.at[n_sems[0]]
        n_sems[0] += 1
        copies = [pltpu.make_async_copy(src, dst, sem) for src, dst in pairs]
        for copy in copies:
            copy.start()
        return copies[0]

    def whole(ref):
        sem = copy_sems.at[n_sems[0] - 1]
        return pltpu.make_async_copy(ref, ref, sem)

    mix_copy = fetch((mix_hbm, mix_s))
    h_width = d // h_chunks
    h_copies = [
        fetch(
            (
                hidden_hbm.at[:, :, pl.ds(c * h_width, h_width)],
                hidden_v.at[:, :, pl.ds(c * h_width, h_width)],
            )
        )
        for c in range(h_chunks)
    ]
    fetch((norm_gain_hbm, norm_v.at[0]), (norm_bias_hbm, norm_v.at[1]))
    norm_copy = whole(norm_v)
    k_depth = d // k_chunks
    in_copies = [
        fetch(
            (
                proj_in_hbm.at[pl.ds(c * k_depth, k_depth), :],
                proj_in_v.at[pl.ds(c * k_depth, k_depth), :],
            )
        )
        for c in range(k_chunks)
    ]
    tok_copy = fetch((tokens_hbm, tokens_s))
    chain_copy = fetch((chain_hbm, chain_s))
    table_copy = fetch((residue_table_hbm, residue_table_v))
    fetch(
        (proj_in_bias_hbm, vec_v.at[0]),
        (proj_out_bias_hbm, vec_v.at[1]),
        (pair_gain_hbm, vec_v.at[2]),
        (pair_bias_hbm, vec_v.at[3]),
    )
    vec_copy = whole(vec_v)
    qk_copies = [fetch((qk_weight_hbm, qk_weight_v)), fetch((qk_bias_hbm, qk_bias_v))]
    o_depth = proj_out_v.shape[0] // o_chunks
    out_copies = [
        fetch(
            (
                proj_out_hbm.at[pl.ds(c * o_depth, o_depth), :],
                proj_out_v.at[pl.ds(c * o_depth, o_depth), :],
            )
        )
        for c in range(o_chunks)
    ]
    pair_copies = [
        fetch((pair_weight_hbm, pair_weight_v)),
        fetch((bins_hbm, bins_v)),
        fetch((relpos_hbm, relpos_v)),
        fetch((chain_table_hbm, chain_table_v)),
    ]

    for step in range(1, n):
        pl.semaphore_signal(
            barrier,
            inc=1,
            device_id={"seq": lax.rem(me + step, n)},
            device_id_type=MESH,
        )

    mix_copy.wait()
    for c in range(h_chunks):
        h_copies[c].wait()
        cols = pl.ds(c * h_width, h_width)
        total = mix_s[0] * hidden_v[0, :, cols].astype(F32)
        for k in range(1, nst):
            total = total + mix_s[k] * hidden_v[k, :, cols].astype(F32)
        mixture_v[:, cols] = total

    norm_copy.wait()
    normed = layer_norm(mixture_v[...], as_row(norm_v[0]), as_row(norm_v[1])).astype(BF16)

    hidden = jnp.zeros((tok, proj_in_v.shape[1]), F32)
    for c in range(k_chunks):
        in_copies[c].wait()
        hidden = hidden + jnp.dot(
            normed[:, c * k_depth : (c + 1) * k_depth],
            proj_in_v[pl.ds(c * k_depth, k_depth), :],
            preferred_element_type=F32,
        )
    tok_copy.wait()
    chain_copy.wait()
    table_copy.wait()
    for i in range(tok):
        residue_v[pl.ds(i, 1), :] = residue_table_v[pl.ds(tokens_s[i], 1), :]
    vec_copy.wait()
    for copy in qk_copies:
        copy.wait()
    hidden = jnp.maximum(hidden + vec_v[0], 0.0).astype(BF16)
    gain = vec_v[2]
    qk_weight = qk_weight_v[...]
    affine = sum_three(
        jnp.dot(
            split_three(
                jnp.concatenate(
                    [jnp.broadcast_to(gain, (8,) + gain.shape[1:]), jnp.broadcast_to(vec_v[3], (8,) + gain.shape[1:])],
                    axis=0,
                )
            ),
            qk_weight,
            preferred_element_type=F32,
        )
    )
    gain_w = affine[0:1]
    bias_w = affine[8:9] + qk_bias_v[...]
    single_f = vec_v[1] + residue_v[...]
    for c in range(o_chunks):
        out_copies[c].wait()
        single_f = single_f + jnp.dot(
            hidden[:, c * o_depth : (c + 1) * o_depth],
            proj_out_v[pl.ds(c * o_depth, o_depth), :],
            preferred_element_type=F32,
        )
    raw = jnp.dot(split_three(single_f * gain), qk_weight, preferred_element_type=F32)
    mean = jnp.mean(single_f, axis=-1, keepdims=True)
    center = single_f - mean
    scale = lax.rsqrt(jnp.mean(center * center, axis=-1, keepdims=True) + epsilon)
    query_key = (sum_three(raw) - mean * gain_w) * scale + bias_w

    span = (LANES - inner) // 2
    lane = lax.broadcasted_iota(jnp.int32, (tok, LANES), 1)
    chains = column_of(chain_s, tok, (tok, LANES))
    onehot = jnp.where(
        (lane == chains + inner) | (lane == chains + (inner + span)), 1.0, 0.0
    ).astype(F32)
    q_rows = jnp.where(lane < inner, query_key, onehot).astype(BF16)
    keys_v[me] = jnp.where(
        lane < inner, pltpu.roll(query_key, LANES - inner, 1), onehot
    ).astype(BF16)

    pl.semaphore_wait(barrier, n - 1)
    for place in range(n):
        target = jnp.where(2 * me >= n, place, n - 1 - place)

        @pl.when(target != me)
        def _():
            pltpu.make_async_remote_copy(
                src_ref=keys_v.at[me],
                dst_ref=keys_v.at[me],
                send_sem=send_sem,
                recv_sem=recv_sems.at[me // per],
                device_id={"seq": target},
                device_id_type=MESH,
            ).start()

    q_ref[...] = q_rows
    single_ref[...] = single_f.astype(BF16)
    for copy in pair_copies:
        copy.wait()
    pair_weight = pair_weight_v[...]
    low_weight = pair_weight[inner:]
    row_diff = jnp.dot(q_rows[:, :inner], low_weight, preferred_element_type=F32)
    chain_base = chain_table_v[pl.ds(0, 1), :]
    chain_hi, chain_lo = split_hi_lo(chain_table_v[pl.ds(1, 1), :] - chain_base)
    weight = jnp.concatenate(
        [
            pair_weight[:inner],
            jnp.broadcast_to(chain_hi, (span, cz)),
            jnp.broadcast_to(chain_lo, (span, cz)),
            -low_weight,
            jnp.zeros((LANES - inner, cz), BF16),
        ],
        axis=0,
    )
    weight_ref[...] = weight
    tables_v[...] = jnp.zeros_like(tables_v)
    hi, lo = split_hi_lo(relpos_v[...])
    tables_v[pl.ds(0, nbins), :] = hi
    tables_v[pl.ds(nbins_pad, nbins), :] = lo
    tables = tables_v[...]
    row_base = row_diff + chain_base
    bins = jnp.concatenate(
        [bins_v[...], jnp.zeros((LANES - tok, length), jnp.int32)], axis=0
    )
    bins_t = bins.T
    bin_lane = lax.broadcasted_iota(jnp.int32, (length, nbins_pad), 1)
    for i in range(tok):
        hot = jnp.where(bins_t[:, i : i + 1] == bin_lane, 1.0, 0.0).astype(BF16)
        base = (
            jnp.dot(
                jnp.concatenate([hot, hot], axis=1), tables, preferred_element_type=F32
            )
            + row_base[i : i + 1]
        )
        base_v[i] = base[:first]
        base_ref[i] = base[first:]

    def arrived(part, count):
        block = keys_v.at[pl.ds(part * per, count)]
        pltpu.make_async_remote_copy(
            src_ref=block,
            dst_ref=block,
            send_sem=send_sem,
            recv_sem=recv_sems.at[part],
            device_id={"seq": lax.rem(me + 1, n)},
            device_id_type=MESH,
        ).wait_recv()

    for part in range(parts):
        own = me // per == part

        @pl.when(jnp.logical_not(own))
        def _():
            arrived(part, per)

        if per > 1:

            @pl.when(own)
            def _():
                arrived(part, per - 1)

        keys = keys_v[pl.ds(part * per, per)].reshape(width, LANES)
        if part == parts - 1:
            last_keys_ref[...] = keys
        else:
            block = pair_block(keys, q_rows, weight, range(tok))
            for i in range(tok):
                pair_ref[i, pl.ds(part * width, width), :] = (
                    block[i * width : (i + 1) * width]
                    + base_v[i, pl.ds(part * width, width), :]
                ).astype(BF16)
    sent = keys_v.at[pl.ds(0, n - 1)]
    pltpu.make_async_remote_copy(
        src_ref=sent,
        dst_ref=sent,
        send_sem=send_sem,
        recv_sem=recv_sems.at[0],
        device_id={"seq": lax.rem(me + 1, n)},
        device_id_type=MESH,
    ).wait_send()


def finish(
    single_ref, pair_ref, base_ref, keys_ref, q_ref, weight_ref,
    single_hbm, pair_hbm, last_v, sems,
):
    tok, width, cz = base_ref.shape
    first = pair_ref.shape[1]
    copies = []

    def put(src, dst):
        copies.append(pltpu.make_async_copy(src, dst, sems.at[len(copies)]))
        copies[-1].start()

    put(pair_ref, pair_hbm.at[:, pl.ds(0, first), :])
    put(single_ref, single_hbm)
    halves = 2
    rows = tok // halves
    for h in range(halves):
        block = pair_block(
            keys_ref[...], q_ref[...], weight_ref[...], range(h * rows, (h + 1) * rows)
        )
        for i in range(rows):
            last_v[h * rows + i] = (
                block[i * width : (i + 1) * width] + base_ref[h * rows + i]
            ).astype(BF16)
        put(
            last_v.at[pl.ds(h * rows, rows)],
            pair_hbm.at[pl.ds(h * rows, rows), pl.ds(first, width), :],
        )
    for copy in copies:
        copy.wait()


def shards(n, *args):
    (hidden, mix, norm_gain, norm_bias, proj_in, proj_in_bias, proj_out, proj_out_bias,
     tokens, residue_table, pair_gain, pair_bias, qk_weight, qk_bias, pair_weight,
     bins, relpos, chain, chain_table) = args
    row = lambda a: a.reshape(1, a.shape[0])
    tiles = lambda a: a.reshape(a.shape[0] // LANES, LANES)
    args = (hidden, mix, tiles(norm_gain), tiles(norm_bias), proj_in, row(proj_in_bias),
            proj_out, row(proj_out_bias), tokens, residue_table, row(pair_gain),
            row(pair_bias), qk_weight, row(qk_bias), pair_weight, bins, relpos, chain,
            chain_table)
    args = tuple(pltpu.with_memory_space_constraint(a, pltpu.HBM) for a in args)
    nst, tok, d = hidden.shape
    cs = proj_out.shape[1]
    cz = pair_weight.shape[1]
    length = bins.shape[1]
    like = lambda a: pltpu.VMEM(a.shape, a.dtype)
    scalars = lambda a: pltpu.SMEM(a.shape, a.dtype)
    nbins_pad = -(-relpos.shape[0] // LANES) * LANES
    h_chunks = k_chunks = 5 if d % (5 * LANES) == 0 else 1
    o_chunks = 4 if proj_out.shape[0] % (4 * LANES) == 0 else 1
    n_copies = 14 + h_chunks + k_chunks + o_chunks
    parts = 8 if n % 8 == 0 else 2
    width = length // parts
    first = length - width
    vmem = pl.BlockSpec(memory_space=pltpu.VMEM)
    hbm = pl.BlockSpec(memory_space=pltpu.HBM)
    mid = pl.pallas_call(
        functools.partial(kernel, n, parts, h_chunks, k_chunks, o_chunks),
        out_shape=(
            jax.ShapeDtypeStruct((tok, cs), BF16),
            jax.ShapeDtypeStruct((tok, first, cz), BF16),
            jax.ShapeDtypeStruct((tok, width, cz), F32),
            jax.ShapeDtypeStruct((width, LANES), BF16),
            jax.ShapeDtypeStruct((tok, LANES), BF16),
            jax.ShapeDtypeStruct((2 * LANES, cz), BF16),
        ),
        in_specs=[hbm] * len(args),
        out_specs=(vmem,) * 6,
        scratch_shapes=[
            like(hidden),
            scalars(mix),
            pltpu.VMEM((2, d // LANES, LANES), F32),
            like(proj_in),
            pltpu.VMEM((4, 1, cs), F32),
            like(proj_out),
            scalars(tokens),
            like(residue_table),
            like(qk_weight),
            pltpu.VMEM((1, qk_bias.shape[0]), F32),
            like(pair_weight),
            like(bins),
            like(relpos),
            scalars(chain),
            like(chain_table),
            pltpu.VMEM((tok, d), F32),
            pltpu.VMEM((tok, cs), F32),
            pltpu.VMEM((2 * nbins_pad, cz), BF16),
            pltpu.VMEM((tok, first, cz), F32),
            pltpu.VMEM((n, tok, LANES), BF16),
            pltpu.SemaphoreType.DMA((n_copies,)),
            pltpu.SemaphoreType.DMA,
            pltpu.SemaphoreType.DMA((parts,)),
        ],
        compiler_params=pltpu.CompilerParams(
            collective_id=0, has_side_effects=True, vmem_limit_bytes=40 << 20
        ),
    )(*args)
    return pl.pallas_call(
        finish,
        out_shape=(
            jax.ShapeDtypeStruct((tok, cs), BF16),
            jax.ShapeDtypeStruct((tok, length, cz), BF16),
        ),
        in_specs=[vmem] * 6,
        out_specs=(hbm, hbm),
        scratch_shapes=[
            pltpu.VMEM((tok, width, cz), BF16),
            pltpu.SemaphoreType.DMA((4,)),
        ],
        compiler_params=pltpu.CompilerParams(vmem_limit_bytes=16 << 20),
    )(*mid)


def solution(mesh):
    in_specs = (
        P(None, ("groups", "seq"), None),
        P(),
        P(),
        P(),
        P(),
        P(),
        P(),
        P(),
        P(("groups", "seq")),
        P(),
        P(),
        P(),
        P(),
        P(),
        P(),
        P(("groups", "seq"), None),
        P(),
        P(("groups", "seq")),
        P(),
    )
    out_specs = (P(("groups", "seq"), None), P(("groups", "seq"), None, None))
    return jax.shard_map(
        functools.partial(shards, mesh.shape["seq"]),
        mesh=mesh,
        in_specs=in_specs,
        out_specs=out_specs,
        check_vma=False,
    )
```

time: 14.7 us -> 14.4 us (0.980)
  Pallas kernels: 13.8 us -> 13.6 us
    pallas_call x1, Pallas kernels: 12.8 us -> 12.6 us  [shards(): pl.pallas_call(functools.partial(kernel, n, parts, h_chunks, k_chunks, o_...]
where the time goes in v1:
time: 14.4 us; the launch traced here: 14.2 us
  Pallas kernels  13.6 us (94%)
  between operations  0.65 us (5%)
    pallas_call x1, Pallas kernels, shards(): pl.pallas_call(functools.partial(kernel, n, parts, h_chunks, k_chunks, o_...  12.6 us
    pallas_call x1, Pallas kernels, shards(): pl.pallas_call(finish, out_shape=(jax.ShapeDtypeStruct((tok, cs), BF16),...  1 us

profile of v1, /device:TPU:0, one launch (start us, length us, event | category | flops | bytes accessed | tf_op | source)
XLA Modules:
  0.0 14.2 jit_solution(1755695418816023707)
XLA Ops:
  0.6 12.6 %shard_map.194 = (bf16[16,1024]{1,0:T(8,128)(2,1)S(1)}, bf16[16,224,128]{2,1,0:T(8,128)(2,1)S(1)}, f32[16,32,128]{2,1,0:T(8,128)S(1)}, bf16[32,128]{1,0:T(8,128)...) custom-call(bf16[37,16,2560]{2,1,0:T(8,128)(2,1)} %hidden_hbm.1, f32[37]{0:T(128)} %mix_hbm.1, ...), custom_call_target="tpu_custom_call" | custom-call | tf_op jit(solution)/shard_map/pallas_call | solution.py:428
  13.2 1.0 %shard_map.195 = (bf16[16,1024]{1,0:T(8,128)(2,1)}, bf16[16,256,128]{2,1,0:T(8,128)(2,1)}) custom-call(bf16[16,1024]{1,0:T(8,128)(2,1)S(1)} %get-tuple-element.8.single_ref, bf16[16,224,128]{2,1,0:T(8,128)(2,1)S(1)} %get-tuple-element.9.pair_ref, f32[16,32,128]{2,1,0:T(8,128)S(1)} %get-tuple-element.10.base_ref, ...), custom_call_target="tpu_custom_call" | custom-call | tf_op jit(solution)/shard_map/pallas_call | solution.py:469

commit v2 on v1

--- a/solution.py
+++ b/solution.py
@@ -62,6 +62,7 @@
     h_chunks,
     k_chunks,
     o_chunks,
+    n_copies,
     hidden_hbm,
     mix_hbm,
     norm_gain_hbm,
@@ -107,7 +108,6 @@
     tables_v,
     base_v,
     keys_v,
-    copy_sems,
     send_sem,
     recv_sems,
 ):
@@ -122,205 +122,212 @@
     per = n // parts
     width = per * tok
     first = length - width
-    n_sems = [0]
-
-    def fetch(*pairs):
-        sem = copy_sems.at[n_sems[0]]
-        n_sems[0] += 1
-        copies = [pltpu.make_async_copy(src, dst, sem) for src, dst in pairs]
-        for copy in copies:
-            copy.start()
-        return copies[0]
-
-    def whole(ref):
-        sem = copy_sems.at[n_sems[0] - 1]
-        return pltpu.make_async_copy(ref, ref, sem)
-
-    mix_copy = fetch((mix_hbm, mix_s))
-    h_width = d // h_chunks
-    h_copies = [
+    def produce(copy_sems):
+        n_sems = [0]
+
+        def fetch(*pairs):
+            sem = copy_sems.at[n_sems[0]]
+            n_sems[0] += 1
+            copies = [pltpu.make_async_copy(src, dst, sem) for src, dst in pairs]
+            for copy in copies:
+                copy.start()
+            return copies[0]
+
+        def whole(ref):
+            sem = copy_sems.at[n_sems[0] - 1]
+            return pltpu.make_async_copy(ref, ref, sem)
+
+        mix_copy = fetch((mix_hbm, mix_s))
+        h_width = d // h_chunks
+        h_copies = [
+            fetch(
+                (
+                    hidden_hbm.at[:, :, pl.ds(c * h_width, h_width)],
+                    hidden_v.at[:, :, pl.ds(c * h_width, h_width)],
+                )
+            )
+            for c in range(h_chunks)
+        ]
+        fetch((norm_gain_hbm, norm_v.at[0]), (norm_bias_hbm, norm_v.at[1]))
+        norm_copy = whole(norm_v)
+        k_depth = d // k_chunks
+        tok_copy = fetch((tokens_hbm, tokens_s))
+        chain_copy = fetch((chain_hbm, chain_s))
+        table_copy = fetch((residue_table_hbm, residue_table_v))
         fetch(
-            (
-                hidden_hbm.at[:, :, pl.ds(c * h_width, h_width)],
-                hidden_v.at[:, :, pl.ds(c * h_width, h_width)],
-            )
+            (proj_in_bias_hbm, vec_v.at[0]),
+            (proj_out_bias_hbm, vec_v.at[1]),
+            (pair_gain_hbm, vec_v.at[2]),
+            (pair_bias_hbm, vec_v.at[3]),
         )
-        for c in range(h_chunks)
-    ]
-    fetch((norm_gain_hbm, norm_v.at[0]), (norm_bias_hbm, norm_v.at[1]))
-    norm_copy = whole(norm_v)
-    k_depth = d // k_chunks
-    in_copies = [
-        fetch(
-            (
-                proj_in_hbm.at[pl.ds(c * k_depth, k_depth), :],
-                proj_in_v.at[pl.ds(c * k_depth, k_depth), :],
-            )
+        vec_copy = whole(vec_v)
+        qk_copies = [fetch((qk_weight_hbm, qk_weight_v)), fetch((qk_bias_hbm, qk_bias_v))]
+        in_copies = [
+            fetch(
+                (
+                    proj_in_hbm.at[pl.ds(c * k_depth, k_depth), :],
+                    proj_in_v.at[pl.ds(c * k_depth, k_depth), :],
+                )
+            )
+            for c in range(k_chunks)
+        ]
+        o_depth = proj_out_v.shape[0] // o_chunks
+        out_copies = [
+            fetch(
+                (
+                    proj_out_hbm.at[pl.ds(c * o_depth, o_depth), :],
+                    proj_out_v.at[pl.ds(c * o_depth, o_depth), :],
+                )
+            )
+            for c in range(o_chunks)
+        ]
+
+        for step in range(1, n):
+            pl.semaphore_signal(
+                barrier,
+                inc=1,
+                device_id={"seq": lax.rem(me + step, n)},
+                device_id_type=MESH,
+            )
+
+        mix_copy.wait()
+        for c in range(h_chunks):
+            h_copies[c].wait()
+            cols = pl.ds(c * h_width, h_width)
+            total = mix_s[0] * hidden_v[0, :, cols].astype(F32)
+            for k in range(1, nst):
+                total = total + mix_s[k] * hidden_v[k, :, cols].astype(F32)
+            mixture_v[:, cols] = total
+
+        norm_copy.wait()
+        normed = layer_norm(mixture_v[...], as_row(norm_v[0]), as_row(norm_v[1])).astype(BF16)
+
+        hidden = jnp.zeros((tok, proj_in_v.shape[1]), F32)
+        for c in range(k_chunks):
+            in_copies[c].wait()
+            hidden = hidden + jnp.dot(
+                normed[:, c * k_depth : (c + 1) * k_depth],
+                proj_in_v[pl.ds(c * k_depth, k_depth), :],
+                preferred_element_type=F32,
+            )
+            if c == 0:
+                tok_copy.wait()
+                chain_copy.wait()
+                table_copy.wait()
+                for i in range(tok):
+                    residue_v[pl.ds(i, 1), :] = residue_table_v[pl.ds(tokens_s[i], 1), :]
+                span = (LANES - inner) // 2
+                lane = lax.broadcasted_iota(jnp.int32, (tok, LANES), 1)
+                chains = column_of(chain_s, tok, (tok, LANES))
+                onehot = jnp.where(
+                    (lane == chains + inner) | (lane == chains + (inner + span)), 1.0, 0.0
+                ).astype(F32)
+            if c == min(1, k_chunks - 1):
+                vec_copy.wait()
+                for copy in qk_copies:
+                    copy.wait()
+                gain = vec_v[2]
+                qk_weight = qk_weight_v[...]
+                affine = sum_three(
+                    jnp.dot(
+                        split_three(
+                            jnp.concatenate(
+                                [jnp.broadcast_to(gain, (8,) + gain.shape[1:]), jnp.broadcast_to(vec_v[3], (8,) + gain.shape[1:])],
+                                axis=0,
+                            )
+                        ),
+                        qk_weight,
+                        preferred_element_type=F32,
+                    )
+                )
+                gain_w = affine[0:1]
+                bias_w = affine[8:9] + qk_bias_v[...]
+        hidden = jnp.maximum(hidden + vec_v[0], 0.0).astype(BF16)
+        single_f = vec_v[1] + residue_v[...]
+        for c in range(o_chunks):
+            out_copies[c].wait()
+            single_f = single_f + jnp.dot(
+                hidden[:, c * o_depth : (c + 1) * o_depth],
+                proj_out_v[pl.ds(c * o_depth, o_depth), :],
+                preferred_element_type=F32,
+            )
+        raw = jnp.dot(split_three(single_f * gain), qk_weight, preferred_element_type=F32)
+        mean = jnp.mean(single_f, axis=-1, keepdims=True)
+        center = single_f - mean
+        scale = lax.rsqrt(jnp.mean(center * center, axis=-1, keepdims=True) + epsilon)
+        query_key = (sum_three(raw) - mean * gain_w) * scale + bias_w
+
+        q_rows = jnp.where(lane < inner, query_key, onehot).astype(BF16)
+        keys_v[me] = jnp.where(
+            lane < inner, pltpu.roll(query_key, LANES - inner, 1), onehot
+        ).astype(BF16)
+
+        pl.semaphore_wait(barrier, n - 1)
+        for place in range(n):
+            target = jnp.where(2 * me >= n, place, n - 1 - place)
+
+            @pl.when(target != me)
+            def _():
+                pltpu.make_async_remote_copy(
+                    src_ref=keys_v.at[me],
+                    dst_ref=keys_v.at[me],
+                    send_sem=send_sem,
+                    recv_sem=recv_sems.at[me // per],
+                    device_id={"seq": target},
+                    device_id_type=MESH,
+                ).start()
+
+        pair_copies = [
+            fetch((pair_weight_hbm, pair_weight_v)),
+            fetch((bins_hbm, bins_v)),
+            fetch((relpos_hbm, relpos_v)),
+            fetch((chain_table_hbm, chain_table_v)),
+        ]
+        q_ref[...] = q_rows
+        single_ref[...] = single_f.astype(BF16)
+        for copy in pair_copies:
+            copy.wait()
+        pair_weight = pair_weight_v[...]
+        low_weight = pair_weight[inner:]
+        row_diff = jnp.dot(q_rows[:, :inner], low_weight, preferred_element_type=F32)
+        chain_base = chain_table_v[pl.ds(0, 1), :]
+        chain_hi, chain_lo = split_hi_lo(chain_table_v[pl.ds(1, 1), :] - chain_base)
+        weight = jnp.concatenate(
+            [
+                pair_weight[:inner],
+                jnp.broadcast_to(chain_hi, (span, cz)),
+                jnp.broadcast_to(chain_lo, (span, cz)),
+                -low_weight,
+                jnp.zeros((LANES - inner, cz), BF16),
+            ],
+            axis=0,
         )
-        for c in range(k_chunks)
-    ]
-    tok_copy = fetch((tokens_hbm, tokens_s))
-    chain_copy = fetch((chain_hbm, chain_s))
-    table_copy = fetch((residue_table_hbm, residue_table_v))
-    fetch(
-        (proj_in_bias_hbm, vec_v.at[0]),
-        (proj_out_bias_hbm, vec_v.at[1]),
-        (pair_gain_hbm, vec_v.at[2]),
-        (pair_bias_hbm, vec_v.at[3]),
-    )
-    vec_copy = whole(vec_v)
-    qk_copies = [fetch((qk_weight_hbm, qk_weight_v)), fetch((qk_bias_hbm, qk_bias_v))]
-    o_depth = proj_out_v.shape[0] // o_chunks
-    out_copies = [
-        fetch(
-            (
-                proj_out_hbm.at[pl.ds(c * o_depth, o_depth), :],
-                proj_out_v.at[pl.ds(c * o_depth, o_depth), :],
-            )
+        weight_ref[...] = weight
+        tables_v[...] = jnp.zeros_like(tables_v)
+        hi, lo = split_hi_lo(relpos_v[...])
+        tables_v[pl.ds(0, nbins), :] = hi
+        tables_v[pl.ds(nbins_pad, nbins), :] = lo
+        tables = tables_v[...]
+        row_base = row_diff + chain_base
+        bins = jnp.concatenate(
+            [bins_v[...], jnp.zeros((LANES - tok, length), jnp.int32)], axis=0
         )
-        for c in range(o_chunks)
-    ]
-    pair_copies = [
-        fetch((pair_weight_hbm, pair_weight_v)),
-        fetch((bins_hbm, bins_v)),
-        fetch((relpos_hbm, relpos_v)),
-        fetch((chain_table_hbm, chain_table_v)),
-    ]
-
-    for step in range(1, n):
-        pl.semaphore_signal(
-            barrier,
-            inc=1,
-            device_id={"seq": lax.rem(me + step, n)},
-            device_id_type=MESH,
-        )
-
-    mix_copy.wait()
-    for c in range(h_chunks):
-        h_copies[c].wait()
-        cols = pl.ds(c * h_width, h_width)
-        total = mix_s[0] * hidden_v[0, :, cols].astype(F32)
-        for k in range(1, nst):
-            total = total + mix_s[k] * hidden_v[k, :, cols].astype(F32)
-        mixture_v[:, cols] = total
-
-    norm_copy.wait()
-    normed = layer_norm(mixture_v[...], as_row(norm_v[0]), as_row(norm_v[1])).astype(BF16)
-
-    hidden = jnp.zeros((tok, proj_in_v.shape[1]), F32)
-    for c in range(k_chunks):
-        in_copies[c].wait()
-        hidden = hidden + jnp.dot(
-            normed[:, c * k_depth : (c + 1) * k_depth],
-            proj_in_v[pl.ds(c * k_depth, k_depth), :],
-            preferred_element_type=F32,
-        )
-    tok_copy.wait()
-    chain_copy.wait()
-    table_copy.wait()
-    for i in range(tok):
-        residue_v[pl.ds(i, 1), :] = residue_table_v[pl.ds(tokens_s[i], 1), :]
-    vec_copy.wait()
-    for copy in qk_copies:
-        copy.wait()
-    hidden = jnp.maximum(hidden + vec_v[0], 0.0).astype(BF16)
-    gain = vec_v[2]
-    qk_weight = qk_weight_v[...]
-    affine = sum_three(
-        jnp.dot(
-            split_three(
-                jnp.concatenate(
-                    [jnp.broadcast_to(gain, (8,) + gain.shape[1:]), jnp.broadcast_to(vec_v[3], (8,) + gain.shape[1:])],
-                    axis=0,
+        bins_t = bins.T
+        bin_lane = lax.broadcasted_iota(jnp.int32, (length, nbins_pad), 1)
+        for i in range(tok):
+            hot = jnp.where(bins_t[:, i : i + 1] == bin_lane, 1.0, 0.0).astype(BF16)
+            base = (
+                jnp.dot(
+                    jnp.concatenate([hot, hot], axis=1), tables, preferred_element_type=F32
                 )
-            ),
-            qk_weight,
-            preferred_element_type=F32,
-        )
-    )
-    gain_w = affine[0:1]
-    bias_w = affine[8:9] + qk_bias_v[...]
-    single_f = vec_v[1] + residue_v[...]
-    for c in range(o_chunks):
-        out_copies[c].wait()
-        single_f = single_f + jnp.dot(
-            hidden[:, c * o_depth : (c + 1) * o_depth],
-            proj_out_v[pl.ds(c * o_depth, o_depth), :],
-            preferred_element_type=F32,
-        )
-    raw = jnp.dot(split_three(single_f * gain), qk_weight, preferred_element_type=F32)
-    mean = jnp.mean(single_f, axis=-1, keepdims=True)
-    center = single_f - mean
-    scale = lax.rsqrt(jnp.mean(center * center, axis=-1, keepdims=True) + epsilon)
-    query_key = (sum_three(raw) - mean * gain_w) * scale + bias_w
-
-    span = (LANES - inner) // 2
-    lane = lax.broadcasted_iota(jnp.int32, (tok, LANES), 1)
-    chains = column_of(chain_s, tok, (tok, LANES))
-    onehot = jnp.where(
-        (lane == chains + inner) | (lane == chains + (inner + span)), 1.0, 0.0
-    ).astype(F32)
-    q_rows = jnp.where(lane < inner, query_key, onehot).astype(BF16)
-    keys_v[me] = jnp.where(
-        lane < inner, pltpu.roll(query_key, LANES - inner, 1), onehot
-    ).astype(BF16)
-
-    pl.semaphore_wait(barrier, n - 1)
-    for place in range(n):
-        target = jnp.where(2 * me >= n, place, n - 1 - place)
-
-        @pl.when(target != me)
-        def _():
-            pltpu.make_async_remote_copy(
-                src_ref=keys_v.at[me],
-                dst_ref=keys_v.at[me],
-                send_sem=send_sem,
-                recv_sem=recv_sems.at[me // per],
-                device_id={"seq": target},
-                device_id_type=MESH,
-            ).start()
-
-    q_ref[...] = q_rows
-    single_ref[...] = single_f.astype(BF16)
-    for copy in pair_copies:
-        copy.wait()
-    pair_weight = pair_weight_v[...]
-    low_weight = pair_weight[inner:]
-    row_diff = jnp.dot(q_rows[:, :inner], low_weight, preferred_element_type=F32)
-    chain_base = chain_table_v[pl.ds(0, 1), :]
-    chain_hi, chain_lo = split_hi_lo(chain_table_v[pl.ds(1, 1), :] - chain_base)
-    weight = jnp.concatenate(
-        [
-            pair_weight[:inner],
-            jnp.broadcast_to(chain_hi, (span, cz)),
-            jnp.broadcast_to(chain_lo, (span, cz)),
-            -low_weight,
-            jnp.zeros((LANES - inner, cz), BF16),
-        ],
-        axis=0,
-    )
-    weight_ref[...] = weight
-    tables_v[...] = jnp.zeros_like(tables_v)
-    hi, lo = split_hi_lo(relpos_v[...])
-    tables_v[pl.ds(0, nbins), :] = hi
-    tables_v[pl.ds(nbins_pad, nbins), :] = lo
-    tables = tables_v[...]
-    row_base = row_diff + chain_base
-    bins = jnp.concatenate(
-        [bins_v[...], jnp.zeros((LANES - tok, length), jnp.int32)], axis=0
-    )
-    bins_t = bins.T
-    bin_lane = lax.broadcasted_iota(jnp.int32, (length, nbins_pad), 1)
-    for i in range(tok):
-        hot = jnp.where(bins_t[:, i : i + 1] == bin_lane, 1.0, 0.0).astype(BF16)
-        base = (
-            jnp.dot(
-                jnp.concatenate([hot, hot], axis=1), tables, preferred_element_type=F32
-            )
-            + row_base[i : i + 1]
-        )
-        base_v[i] = base[:first]
-        base_ref[i] = base[first:]
+                + row_base[i : i + 1]
+            )
+            base_v[i] = base[:first]
+            base_ref[i] = base[first:]
+
+    pl.run_scoped(produce, pltpu.SemaphoreType.DMA((n_copies,)))
+    q_rows = q_ref[...]
+    weight = weight_ref[...]
 
     def arrived(part, count):
         block = keys_v.at[pl.ds(part * per, count)]
@@ -417,7 +424,7 @@
     like = lambda a: pltpu.VMEM(a.shape, a.dtype)
     scalars = lambda a: pltpu.SMEM(a.shape, a.dtype)
     nbins_pad = -(-relpos.shape[0] // LANES) * LANES
-    h_chunks = k_chunks = 5 if d % (5 * LANES) == 0 else 1
+    h_chunks, k_chunks = (5, 10) if d % (10 * LANES) == 0 else (1, 1)
     o_chunks = 4 if proj_out.shape[0] % (4 * LANES) == 0 else 1
     n_copies = 14 + h_chunks + k_chunks + o_chunks
     parts = 8 if n % 8 == 0 else 2
@@ -426,7 +433,7 @@
     vmem = pl.BlockSpec(memory_space=pltpu.VMEM)
     hbm = pl.BlockSpec(memory_space=pltpu.HBM)
     mid = pl.pallas_call(
-        functools.partial(kernel, n, parts, h_chunks, k_chunks, o_chunks),
+        functools.partial(kernel, n, parts, h_chunks, k_chunks, o_chunks, n_copies),
         out_shape=(
             jax.ShapeDtypeStruct((tok, cs), BF16),
             jax.ShapeDtypeStruct((tok, first, cz), BF16),
@@ -458,7 +465,6 @@
             pltpu.VMEM((2 * nbins_pad, cz), BF16),
             pltpu.VMEM((tok, first, cz), F32),
             pltpu.VMEM((n, tok, LANES), BF16),
-            pltpu.SemaphoreType.DMA((n_copies,)),
             pltpu.SemaphoreType.DMA,
             pltpu.SemaphoreType.DMA((parts,)),
         ],

time: 14.4 us -> 14.1 us (0.979)
  Pallas kernels: 13.6 us -> 13.3 us
    pallas_call x1, Pallas kernels: 12.6 us -> 12.3 us  [shards(): pl.pallas_call(functools.partial(kernel, n, parts, h_chunks, k_chunks, o_...]
where the time goes in v2:
time: 14.1 us; the launch traced here: 13.9 us
  Pallas kernels  13.3 us (94%)
  between operations  0.65 us (5%)
    pallas_call x1, Pallas kernels, shards(): pl.pallas_call(functools.partial(kernel, n, parts, h_chunks, k_chunks, o_...  12.3 us
    pallas_call x1, Pallas kernels, shards(): pl.pallas_call(finish, out_shape=(jax.ShapeDtypeStruct((tok, cs), BF16),...  1 us

profile of v2, /device:TPU:0, one launch (start us, length us, event | category | flops | bytes accessed | tf_op | source)
XLA Modules:
  0.0 13.9 jit_solution(13562259563378301516)
XLA Ops:
  0.6 12.3 %shard_map.194 = (bf16[16,1024]{1,0:T(8,128)(2,1)S(1)}, bf16[16,224,128]{2,1,0:T(8,128)(2,1)S(1)}, f32[16,32,128]{2,1,0:T(8,128)S(1)}, bf16[32,128]{1,0:T(8,128)...) custom-call(bf16[37,16,2560]{2,1,0:T(8,128)(2,1)} %hidden_hbm.1, f32[37]{0:T(128)} %mix_hbm.1, ...), custom_call_target="tpu_custom_call" | custom-call | tf_op jit(solution)/shard_map/pallas_call | solution.py:435
  12.9 1.0 %shard_map.195 = (bf16[16,1024]{1,0:T(8,128)(2,1)}, bf16[16,256,128]{2,1,0:T(8,128)(2,1)}) custom-call(bf16[16,1024]{1,0:T(8,128)(2,1)S(1)} %get-tuple-element.8.single_ref, bf16[16,224,128]{2,1,0:T(8,128)(2,1)S(1)} %get-tuple-element.9.pair_ref, f32[16,32,128]{2,1,0:T(8,128)S(1)} %get-tuple-element.10.base_ref, ...), custom_call_target="tpu_custom_call" | custom-call | tf_op jit(solution)/shard_map/pallas_call | solution.py:475

commit v3 on v2

--- a/solution.py
+++ b/solution.py
@@ -32,6 +32,10 @@
     mid = rest.astype(BF16)
     low = (rest - mid.astype(F32)).astype(BF16)
     return jnp.concatenate([hi, mid, low], axis=0)
+
+
+def split_rows(values):
+    return jnp.concatenate(split_hi_lo(values), axis=0)
 
 
 def sum_three(stacked):
@@ -122,6 +126,10 @@
     per = n // parts
     width = per * tok
     first = length - width
+
+    def group_of(source):
+        return jnp.maximum(source - n // 2 + per, 0) // per
+
     def produce(copy_sems):
         n_sems = [0]
 
@@ -251,11 +259,11 @@
                 proj_out_v[pl.ds(c * o_depth, o_depth), :],
                 preferred_element_type=F32,
             )
-        raw = jnp.dot(split_three(single_f * gain), qk_weight, preferred_element_type=F32)
+        raw = jnp.dot(split_rows(single_f * gain), qk_weight, preferred_element_type=F32)
         mean = jnp.mean(single_f, axis=-1, keepdims=True)
         center = single_f - mean
         scale = lax.rsqrt(jnp.mean(center * center, axis=-1, keepdims=True) + epsilon)
-        query_key = (sum_three(raw) - mean * gain_w) * scale + bias_w
+        query_key = (raw[:tok] + raw[tok:] - mean * gain_w) * scale + bias_w
 
         q_rows = jnp.where(lane < inner, query_key, onehot).astype(BF16)
         keys_v[me] = jnp.where(
@@ -272,7 +280,7 @@
                     src_ref=keys_v.at[me],
                     dst_ref=keys_v.at[me],
                     send_sem=send_sem,
-                    recv_sem=recv_sems.at[me // per],
+                    recv_sem=recv_sems.at[group_of(me)],
                     device_id={"seq": target},
                     device_id_type=MESH,
                 ).start()
@@ -329,29 +337,32 @@
     q_rows = q_ref[...]
     weight = weight_ref[...]
 
-    def arrived(part, count):
-        block = keys_v.at[pl.ds(part * per, count)]
+    def arrived(group, count):
+        block = keys_v.at[pl.ds(0, count)]
         pltpu.make_async_remote_copy(
             src_ref=block,
             dst_ref=block,
             send_sem=send_sem,
-            recv_sem=recv_sems.at[part],
+            recv_sem=recv_sems.at[group],
             device_id={"seq": lax.rem(me + 1, n)},
             device_id_type=MESH,
         ).wait_recv()
 
     for part in range(parts):
-        own = me // per == part
-
-        @pl.when(jnp.logical_not(own))
-        def _():
-            arrived(part, per)
-
-        if per > 1:
-
-            @pl.when(own)
+        if part == 0 or part >= parts // 2:
+            group = max(0, part - parts // 2 + 1)
+            count = n // 2 if part == 0 else per
+            own = group_of(me) == group
+
+            @pl.when(jnp.logical_not(own))
             def _():
-                arrived(part, per - 1)
+                arrived(group, count)
+
+            if count > 1:
+
+                @pl.when(own)
+                def _():
+                    arrived(group, count - 1)
 
         keys = keys_v[pl.ds(part * per, per)].reshape(width, LANES)
         if part == parts - 1:
@@ -466,7 +477,7 @@
             pltpu.VMEM((tok, first, cz), F32),
             pltpu.VMEM((n, tok, LANES), BF16),
             pltpu.SemaphoreType.DMA,
-            pltpu.SemaphoreType.DMA((parts,)),
+            pltpu.SemaphoreType.DMA((parts // 2 + 1,)),
         ],
         compiler_params=pltpu.CompilerParams(
             collective_id=0, has_side_effects=True, vmem_limit_bytes=40 << 20

time: 14.1 us -> 14.1 us (level)
  no operation moved by 1% of the time
where the time goes in v3:
time: 14.1 us; the launch traced here: 13.9 us
  Pallas kernels  13.3 us (94%)
  between operations  0.65 us (5%)
    pallas_call x1, Pallas kernels, shards(): pl.pallas_call(functools.partial(kernel, n, parts, h_chunks, k_chunks, o_...  12.3 us
    pallas_call x1, Pallas kernels, shards(): pl.pallas_call(finish, out_shape=(jax.ShapeDtypeStruct((tok, cs), BF16),...  1 us

profile of v3, /device:TPU:0, one launch (start us, length us, event | category | flops | bytes accessed | tf_op | source)
XLA Modules:
  0.0 13.9 jit_solution(15266236120821688514)
XLA Ops:
  0.6 12.3 %shard_map.194 = (bf16[16,1024]{1,0:T(8,128)(2,1)S(1)}, bf16[16,224,128]{2,1,0:T(8,128)(2,1)S(1)}, f32[16,32,128]{2,1,0:T(8,128)S(1)}, bf16[32,128]{1,0:T(8,128)...) custom-call(bf16[37,16,2560]{2,1,0:T(8,128)(2,1)} %hidden_hbm.1, f32[37]{0:T(128)} %mix_hbm.1, ...), custom_call_target="tpu_custom_call" | custom-call | tf_op jit(solution)/shard_map/pallas_call | solution.py:446
  12.9 1.0 %shard_map.195 = (bf16[16,1024]{1,0:T(8,128)(2,1)}, bf16[16,256,128]{2,1,0:T(8,128)(2,1)}) custom-call(bf16[16,1024]{1,0:T(8,128)(2,1)S(1)} %get-tuple-element.8.single_ref, bf16[16,224,128]{2,1,0:T(8,128)(2,1)S(1)} %get-tuple-element.9.pair_ref, f32[16,32,128]{2,1,0:T(8,128)S(1)} %get-tuple-element.10.base_ref, ...), custom_call_target="tpu_custom_call" | custom-call | tf_op jit(solution)/shard_map/pallas_call | solution.py:486

commit v4 on v3

--- a/solution.py
+++ b/solution.py
@@ -253,6 +253,8 @@
         hidden = jnp.maximum(hidden + vec_v[0], 0.0).astype(BF16)
         single_f = vec_v[1] + residue_v[...]
         for c in range(o_chunks):
+            if c == o_chunks - 1:
+                pl.semaphore_wait(barrier, n - 1)
             out_copies[c].wait()
             single_f = single_f + jnp.dot(
                 hidden[:, c * o_depth : (c + 1) * o_depth],
@@ -270,7 +272,6 @@
             lane < inner, pltpu.roll(query_key, LANES - inner, 1), onehot
         ).astype(BF16)
 
-        pl.semaphore_wait(barrier, n - 1)
         for place in range(n):
             target = jnp.where(2 * me >= n, place, n - 1 - place)
 

time: 14.1 us -> 14.1 us (level)
  no operation moved by 1% of the time
where the time goes in v4:
time: 14.1 us; the launch traced here: 13.9 us
  Pallas kernels  13.3 us (94%)
  between operations  0.65 us (5%)
    pallas_call x1, Pallas kernels, shards(): pl.pallas_call(functools.partial(kernel, n, parts, h_chunks, k_chunks, o_...  12.3 us
    pallas_call x1, Pallas kernels, shards(): pl.pallas_call(finish, out_shape=(jax.ShapeDtypeStruct((tok, cs), BF16),...  1 us

profile of v4, /device:TPU:0, one launch (start us, length us, event | category | flops | bytes accessed | tf_op | source)
XLA Modules:
  0.0 13.9 jit_solution(17606896438732081212)
XLA Ops:
  0.6 12.3 %shard_map.194 = (bf16[16,1024]{1,0:T(8,128)(2,1)S(1)}, bf16[16,224,128]{2,1,0:T(8,128)(2,1)S(1)}, f32[16,32,128]{2,1,0:T(8,128)S(1)}, bf16[32,128]{1,0:T(8,128)...) custom-call(bf16[37,16,2560]{2,1,0:T(8,128)(2,1)} %hidden_hbm.1, f32[37]{0:T(128)} %mix_hbm.1, ...), custom_call_target="tpu_custom_call" | custom-call | tf_op jit(solution)/shard_map/pallas_call | solution.py:447
  12.9 1.0 %shard_map.195 = (bf16[16,1024]{1,0:T(8,128)(2,1)}, bf16[16,256,128]{2,1,0:T(8,128)(2,1)}) custom-call(bf16[16,1024]{1,0:T(8,128)(2,1)S(1)} %get-tuple-element.8.single_ref, bf16[16,224,128]{2,1,0:T(8,128)(2,1)S(1)} %get-tuple-element.9.pair_ref, f32[16,32,128]{2,1,0:T(8,128)S(1)} %get-tuple-element.10.base_ref, ...), custom_call_target="tpu_custom_call" | custom-call | tf_op jit(solution)/shard_map/pallas_call | solution.py:487
